TPU v7x, 128 devices: a whole 4x4x4 slice. The times are simulated.
128 devices in a mesh: grp: 8 (over z, x_hi), dev: 16 (over y, x_lo, core).
Axes of the slice: x: 4 (x_hi: 2, x_lo: 2; x = x_hi * 2 + x_lo), y: 4, z: 4, core: 2. Of those that a mesh axis runs over, the one named last changes fastest.
Arguments:
- output_gradient: bfloat16 [16384, 2048], P(('grp', 'dev')), may hold values from -6 to 6
- expert_choice_index: int32 [16384, 8], P(('grp', 'dev')), may hold values from 0 to 127, all different within a row; in each aligned block of 128 rows (0 to 127, 128 to 255, ...) at most 10 rows name the same one
- routing_weight: float32 [16384, 8], P(('grp', 'dev')), may hold values from 0.05 to 0.3
- stored_gate_preact: bfloat16 [128, 1280, 1536], P(('grp', 'dev')), may hold values from -6 to 6
- gate_up_weight: bfloat16 [128, 2048, 1536], P(('grp', 'dev')), may hold values from -0.125 to 0.125
- down_weight: bfloat16 [128, 768, 2048], P(('grp', 'dev')), may hold values from -0.21875 to 0.21875
- down_first_factor: bfloat16 [128, 64, 768], P(('grp', 'dev')), may hold values from -0.21875 to 0.21875
- down_second_factor: bfloat16 [128, 64, 2048], P(('grp', 'dev')), may hold values from -0.75 to 0.75
- rotated_queries: bfloat16 [16384, 4096], P('grp', 'dev'), may hold values from -800 to 800
- rotated_keys: bfloat16 [16384, 512], P('grp'), may hold values from -4 to 4
- stored_values: bfloat16 [16384, 512], P('grp'), may hold values from -6 to 6
- output_weight: bfloat16 [4096, 2048], P('dev'), may hold values from -0.09375 to 0.09375
- output_first_factor: bfloat16 [64, 4096], P(None, 'dev'), may hold values from -0.09375 to 0.09375
- output_second_factor: bfloat16 [64, 2048], replicated, may hold values from -0.75 to 0.75
Outputs:
- first_factor_gradient: float32 [128, 64, 768], P(('grp', 'dev'))
- second_factor_gradient: float32 [128, 64, 2048], P(('grp', 'dev'))
- residual_gradient: bfloat16 [16384, 2048], P(('grp', 'dev'))
- output_first_gradient: float32 [64, 4096], P(None, 'dev')
- output_second_gradient: float32 [64, 2048], replicated
- query_gradient: float32 [16384, 4096], P('grp', 'dev')
- key_gradient: float32 [16384, 512], P(('grp', 'dev'))
- value_gradient: float32 [16384, 512], P(('grp', 'dev'))
Inputs may be any that keep to these rules, and one draw needn't show every extreme that they name: `expert_choice_index`: each row names 8 different experts; within the rows of one device no expert is named more than 10 times, a bound that some block reaches.
All inputs are finite; a program needn't handle non-finite values.
Results may differ from a plain program's by a relative error of at most 0.024.
Values may be sent and summed in bfloat16 or wider, within the bound.
A program may use at most 192 MiB of HBM per device.

v0:
```python
import jax
import jax.numpy as jnp
from jax import lax
from jax.sharding import PartitionSpec as P

QUERY_HEADS = 32
KVH = 4
HEAD_SIZE = 128
adapter_scale = 2.0
neg_big = -1e30


def contraction(left, right, left_dim, right_dim):
    return lax.dot_general(
        left, right, (((left_dim,), (right_dim,)), ((), ())), preferred_element_type=jnp.float32
    )


def expert_backward(routed_rows, saved_rows, gate_up, down_output, lowrank_first, low_b):
    width_ff = down_output.shape[0]
    pre_gate = saved_rows[:, :width_ff].astype(jnp.float32)
    pre_up = saved_rows[:, width_ff:].astype(jnp.float32)
    sigmoid = jax.nn.sigmoid(pre_gate)
    activated = pre_gate * sigmoid
    slope = sigmoid * (1.0 + pre_gate * (1.0 - sigmoid))
    hidden_activity = (activated * pre_up).astype(jnp.bfloat16)
    lowrank_input = contraction(hidden_activity, lowrank_first, 1, 1).astype(jnp.bfloat16)
    lowrank_gradient = contraction(routed_rows, low_b, 1, 1).astype(jnp.bfloat16)
    gradient_second = adapter_scale * contraction(lowrank_input, routed_rows, 0, 0)
    gradient_first = adapter_scale * contraction(lowrank_gradient, hidden_activity, 0, 0)
    hidden_gradient = contraction(routed_rows, down_output, 1, 1) + adapter_scale * jnp.dot(
        lowrank_gradient, lowrank_first, preferred_element_type=jnp.float32
    )
    grad_pre = jnp.concatenate(
        [hidden_gradient * pre_up * slope, hidden_gradient * activated], axis=1
    ).astype(jnp.bfloat16)
    return (
        contraction(grad_pre, gate_up, 1, 1).astype(jnp.bfloat16),
        gradient_first,
        gradient_second,
    )


def on_device(
    output_gradient,
    expert_choice_index,
    routing_weight,
    stored_gate_preact,
    gate_up_weight,
    down_weight,
    down_first_factor,
    down_second_factor,
    rotated_queries,
    rotated_keys,
    stored_values,
    output_weight,
    output_first_factor,
    output_second_factor,
):
    tok_rows, model_width = output_gradient.shape
    top_count = expert_choice_index.shape[1]
    grp_count = lax.axis_size("grp")
    dev_count = lax.axis_size("dev")
    experts = grp_count * dev_count
    slot_count = stored_gate_preact.shape[1]
    capacity = slot_count // experts
    assign = tok_rows * top_count
    flat_ids = expert_choice_index.reshape(assign)
    onehot = (flat_ids[:, None] == jnp.arange(experts, dtype=jnp.int32)[None, :]).astype(jnp.int32)
    before = jnp.cumsum(onehot, axis=0) - onehot
    slot_rank = jnp.sum(before * onehot, axis=1)
    cells = flat_ids * capacity + slot_rank
    scaled = (
        (routing_weight[:, :, None] * output_gradient[:, None, :].astype(jnp.float32))
        .astype(jnp.bfloat16)
        .reshape(assign, model_width)
    )
    outgoing = jnp.zeros((experts * capacity, model_width), jnp.bfloat16).at[cells].set(scaled)
    outgoing = outgoing.reshape(experts, capacity, model_width)
    incoming = lax.all_to_all(outgoing, ("grp", "dev"), split_axis=0, concat_axis=0, tiled=True)
    routed_rows = incoming.reshape(slot_count, model_width)
    grad_rows, gradient_first, gradient_second = expert_backward(
        routed_rows,
        stored_gate_preact[0],
        gate_up_weight[0],
        down_weight[0],
        down_first_factor[0],
        down_second_factor[0],
    )
    returned = lax.all_to_all(
        grad_rows.reshape(experts, capacity, model_width),
        ("grp", "dev"),
        split_axis=0,
        concat_axis=0,
        tiled=True,
    )
    picked = returned.reshape(experts * capacity, model_width)[cells]
    merged_result = jnp.sum(
        picked.reshape(tok_rows, top_count, model_width).astype(jnp.float32), axis=1
    )
    residual_gradient = (output_gradient.astype(jnp.float32) + merged_result).astype(jnp.bfloat16)
    segment_gradient = lax.all_gather(residual_gradient, "dev", axis=0, tiled=True)
    piece_len = segment_gradient.shape[0]
    device_share = rotated_queries.shape[1] // HEAD_SIZE
    group_size = QUERY_HEADS // KVH
    rank_total = output_second_factor.shape[0]
    kv_index = lax.axis_index("dev") * device_share // group_size
    key_rows = lax.dynamic_slice_in_dim(rotated_keys, kv_index * HEAD_SIZE, HEAD_SIZE, 1)
    value_rows = lax.dynamic_slice_in_dim(stored_values, kv_index * HEAD_SIZE, HEAD_SIZE, 1)
    lowrank_token = contraction(segment_gradient, output_second_factor, 1, 1).astype(jnp.bfloat16)
    head_gradient = (
        contraction(segment_gradient, output_weight, 1, 1)
        + adapter_scale
        * jnp.dot(lowrank_token, output_first_factor, preferred_element_type=jnp.float32)
    ).astype(jnp.bfloat16)
    lowrank_heads = output_first_factor.reshape(rank_total, device_share, HEAD_SIZE)
    att_scale = HEAD_SIZE ** (-0.5)
    block_rows = min(512, piece_len)
    grad_key_sum = jnp.zeros((piece_len, HEAD_SIZE), jnp.float32)
    grad_value_sum = jnp.zeros((piece_len, HEAD_SIZE), jnp.float32)
    row_contrib = jnp.zeros((rank_total, device_share * HEAD_SIZE), jnp.float32)
    column_contrib = jnp.zeros((rank_total, model_width), jnp.float32)
    query_parts = []
    for number in range(piece_len // block_rows):
        first_row = number * block_rows
        last_row = first_row + block_rows
        query_block = rotated_queries[first_row:last_row].reshape(
            block_rows, device_share, HEAD_SIZE
        )
        grad_block = head_gradient[first_row:last_row].reshape(block_rows, device_share, HEAD_SIZE)
        key_part = key_rows[:last_row]
        value_part = value_rows[:last_row]
        scores = (
            jnp.einsum("qhd,kd->hqk", query_block, key_part, preferred_element_type=jnp.float32)
            * att_scale
        )
        positions = first_row + jnp.arange(block_rows, dtype=jnp.int32)
        causal = positions[:, None] >= jnp.arange(last_row, dtype=jnp.int32)[None, :]
        scores = jnp.where(causal[None, :, :], scores, neg_big)
        probs_full = jnp.exp(scores - jnp.max(scores, axis=2, keepdims=True))
        probs_full = probs_full / jnp.sum(probs_full, axis=2, keepdims=True)
        probs_low = probs_full.astype(jnp.bfloat16)
        attended = jnp.einsum(
            "hqk,kd->qhd", probs_low, value_part, preferred_element_type=jnp.float32
        ).astype(jnp.bfloat16)
        grad_probs = jnp.einsum(
            "qhd,kd->hqk", grad_block, value_part, preferred_element_type=jnp.float32
        )
        row_delta = jnp.sum(grad_block.astype(jnp.float32) * attended.astype(jnp.float32), axis=2)
        grad_scores = (probs_full * (grad_probs - row_delta.T[:, :, None])).astype(jnp.bfloat16)
        query_parts.append(
            att_scale
            * jnp.einsum("hqk,kd->qhd", grad_scores, key_part, preferred_element_type=jnp.float32)
        )
        grad_key_sum = grad_key_sum.at[:last_row].add(
            att_scale
            * jnp.einsum(
                "hqk,qhd->kd", grad_scores, query_block, preferred_element_type=jnp.float32
            )
        )
        grad_value_sum = grad_value_sum.at[:last_row].add(
            jnp.einsum("hqk,qhd->kd", probs_low, grad_block, preferred_element_type=jnp.float32)
        )
        row_contrib = row_contrib + contraction(
            lowrank_token[first_row:last_row],
            attended.reshape(block_rows, device_share * HEAD_SIZE),
            0,
            0,
        )
        flattened = jnp.einsum(
            "qhd,rhd->qhr", attended, lowrank_heads, preferred_element_type=jnp.float32
        ).astype(jnp.bfloat16)
        column_contrib = column_contrib + jnp.einsum(
            "qhr,qc->rc",
            flattened,
            segment_gradient[first_row:last_row],
            preferred_element_type=jnp.float32,
        )
    query_gradient = jnp.concatenate(query_parts, axis=0).reshape(
        piece_len, device_share * HEAD_SIZE
    )
    output_first_gradient = lax.psum(
        (adapter_scale * row_contrib).astype(jnp.bfloat16), "grp"
    ).astype(jnp.float32)
    output_second_gradient = lax.psum(adapter_scale * column_contrib, ("grp", "dev"))
    empty = jnp.zeros((piece_len, KVH * HEAD_SIZE), jnp.float32)
    key_term = lax.dynamic_update_slice(empty, grad_key_sum, (0, kv_index * HEAD_SIZE))
    value_term = lax.dynamic_update_slice(empty, grad_value_sum, (0, kv_index * HEAD_SIZE))
    key_gradient, value_gradient = (
        lax.psum_scatter(
            key_term.astype(jnp.bfloat16), "dev", scatter_dimension=0, tiled=True
        ).astype(jnp.float32),
        lax.psum_scatter(
            value_term.astype(jnp.bfloat16), "dev", scatter_dimension=0, tiled=True
        ).astype(jnp.float32),
    )
    return (
        gradient_first[None],
        gradient_second[None],
        residual_gradient,
        output_first_gradient,
        output_second_gradient,
        query_gradient,
        key_gradient,
        value_gradient,
    )


def solution(mesh):
    in_specs = (
        P(("grp", "dev"), None),
        P(("grp", "dev"), None),
        P(("grp", "dev"), None),
        P(("grp", "dev"), None, None),
        P(("grp", "dev"), None, None),
        P(("grp", "dev"), None, None),
        P(("grp", "dev"), None, None),
        P(("grp", "dev"), None, None),
        P("grp", "dev"),
        P("grp", None),
        P("grp", None),
        P("dev", None),
        P(None, "dev"),
        P(),
    )
    out_specs = (
        P(("grp", "dev"), None, None),
        P(("grp", "dev"), None, None),
        P(("grp", "dev"), None),
        P(None, "dev"),
        P(),
        P("grp", "dev"),
        P(("grp", "dev"), None),
        P(("grp", "dev"), None),
    )
    return jax.shard_map(
        on_device, mesh=mesh, in_specs=in_specs, out_specs=out_specs, check_vma=False
    )
```

profile of v0, /device:TPU:1, one launch (start us, length us, event | category | flops | bytes accessed | tf_op | source)
XLA Modules:
  0.0 718.6 jit_solution(16234337022996242933)
XLA Ops:
  16.2 10.5 %scatter_custom_fusion = bf16[1280,2048]{1,0:T(8,128)(2,1)} fusion(s32[1024]{0:T(1024)S(1)} %bitcast.379, f32[128,2048]{1,0:T(8,128)} %convert_element_type.174, f32[1024]{0:T(1024)S(1)} %mul.209, bf16[]{:T(256)} %constant.250.clone.1), kind=kCustom, calls=%fused_computation.28 | custom fusion | flops 4194304 | bytes 6295554 | tf_op jit(solution)/shard_map/scatter | solution.py:78
  26.6 9.5 %reshape.411 = bf16[128,10,2048]{2,1,0:T(8,128)(2,1)} reshape(bf16[1280,2048]{1,0:T(8,128)(2,1)} %scatter_custom_fusion) | data formatting | bytes 10485760 | tf_op jit(solution)/shard_map/reshape | solution.py:79
  36.2 12.4 %all-to-all-start = ((bf16[128,10,2048]{2,1,0:T(8,128)(2,1)}), bf16[128,10,2048]{2,1,0:T(8,128)(2,1)}, u32[]{:S(2)}, u32[]{:S(2)}) async-start(bf16[128,10,2048]{2,1,0:T(8,128)(2,1)} %reshape.411), calls=%async_computation | async-start | bytes 16777216 | tf_op jit(solution)/shard_map/all_to_all | solution.py:80
  48.6 6.2 copy.100
  54.9 94.9 %all-to-all-done = bf16[128,10,2048]{2,1,0:T(8,128)(2,1)} async-done(((bf16[128,10,2048]{2,1,0:T(8,128)(2,1)}), bf16[128,10,2048]{2,1,0:T(8,128)(2,1)}, u32[]{:S(2)}, u32[]{:S(2)}) %all-to-all-start) | async-done | bytes 5242912 | tf_op jit(solution)/shard_map/all_to_all | solution.py:80
  149.8 9.8 %reshape.412 = bf16[1280,2048]{1,0:T(8,128)(2,1)} reshape(bf16[128,10,2048]{2,1,0:T(8,128)(2,1)} %all-to-all-done) | data formatting | bytes 10485760 | tf_op jit(solution)/shard_map/reshape | solution.py:81
  159.6 4.3 convolution_convert_fusion.3
  172.2 10.2 %convolution_convert_fusion = bf16[1280,2048]{1,0:T(8,128)(2,1)} fusion(bf16[1,2048,1536]{2,1,0:T(8,128)(2,1)S(1)} %bitcast.382, bf16[1280,768]{0,1:T(8,128)(2,1)S(1)} %get-tuple-element.149, bf16[1280,768]{0,1:T(8,128)(2,1)S(1)} %get-tuple-element.148), kind=kOutput, calls=%fused_computation.14 | convolution fusion | flops 8063549440 | bytes 15466496 | tf_op jit(solution)/shard_map/dot_general | solution.py:14
  182.4 9.5 %reshape.413 = bf16[128,10,2048]{2,1,0:T(8,128)(2,1)} reshape(bf16[1280,2048]{1,0:T(8,128)(2,1)} %convolution_convert_fusion) | data formatting | bytes 10485760 | tf_op jit(solution)/shard_map/reshape | solution.py:91
  191.9 15.0 %all-to-all-start.1 = ((bf16[128,10,2048]{2,1,0:T(8,128)(2,1)}), bf16[128,10,2048]{2,1,0:T(8,128)(2,1)}, u32[]{:S(2)}, u32[]{:S(2)}) async-start(bf16[128,10,2048]{2,1,0:T(8,128)(2,1)} %reshape.413), calls=%async_computation.1 | async-start | bytes 16777216 | tf_op jit(solution)/shard_map/all_to_all | solution.py:90
  206.9 101.3 %all-to-all-done.1 = bf16[128,10,2048]{2,1,0:T(8,128)(2,1)} async-done(((bf16[128,10,2048]{2,1,0:T(8,128)(2,1)}), bf16[128,10,2048]{2,1,0:T(8,128)(2,1)}, u32[]{:S(2)}, u32[]{:S(2)}) %all-to-all-start.1) | async-done | bytes 5242912 | tf_op jit(solution)/shard_map/all_to_all | solution.py:90
  308.2 9.8 %reshape.414 = bf16[1280,2048]{1,0:T(8,128)(2,1)} reshape(bf16[128,10,2048]{2,1,0:T(8,128)(2,1)} %all-to-all-done.1) | data formatting | bytes 10485760 | tf_op jit(solution)/shard_map/reshape | solution.py:97
  318.1 12.0 %gather_fusion = bf16[1024,2048]{1,0:T(8,128)(2,1)} fusion(bf16[1280,2048]{1,0:T(8,128)(2,1)} %reshape.414, s32[1024]{0:T(1024)S(1)} %broadcast_clamp_fusion), kind=kCustom, calls=%fused_computation | custom fusion | bytes 8392704 | tf_op jit(solution)/shard_map/gather | solution.py:97
  330.0 5.1 convert_reduce_fusion
  336.1 8.8 %reduce-scatter.3.cloned.1.call-start = ((), (), s32[]{:S(2)}) async-start(), calls=%async_computation.6 | async-start | bytes 2228224 | tf_op jit(solution)/shard_map/reduce_scatter | solution.py:190
  351.5 4.6 fusion.177
  364.1 6.1 fusion.178
  378.9 8.2 %fusion.179 = (f32[2,512]{1,0:T(2,128)S(1)}, f32[2,512,2048]{1,2,0:T(8,128)}) fusion(pred[512,2048]{0,1:T(8,128)(4,1)} %iota_compare_fusion, bf16[512,2,128]{0,2,1:T(8,128)(2,1)S(1)} %bitcast.363, bf16[2048,512]{1,0:T(8,128)(2,1)} %param.43, s32[]{:T(128)S(6)} %select_n.40), kind=kOutput, calls=%fused_computation.246 | convolution fusion | flops 545261568 | bytes 10227716 | tf_op jit(solution)/shard_map/sub | solution.py:140
  387.1 4.7 fusion.33
  394.6 6.1 fusion.184
  436.7 5.4 fusion.54
  446.9 38.8 %psum.14 = bf16[64,256]{1,0:T(8,128)(2,1)S(1)} all-reduce(bf16[64,256]{1,0:T(8,128)(2,1)S(1)} %fusion.88), channel_id=1, replica_groups=mesh['grp'=8,'dev'=16] {'grp'}, use_global_device_ids=true, to_apply=%region_13.14 | all-reduce | flops 16384 | bytes 65536 | tf_op jit(solution)/shard_map/psum | solution.py:182
  514.1 42.5 %reduce-scatter.5.cloned.1.call-done = bf16[128,512]{1,0:T(8,128)(2,1)} async-done(((bf16[2048,512]{1,0:T(8,128)(2,1)}), bf16[128,512]{1,0:T(8,128)(2,1)}) %reduce-scatter.5.cloned.1.call-update) | async-done | bytes 131088 | tf_op jit(solution)/shard_map/reduce_scatter | solution.py:193
  558.2 151.8 %all-reduce.4.cloned.1.call-done = f32[64,2048]{1,0:T(8,128)} async-done(((f32[64,2048]{1,0:T(8,128)}), f32[64,2048]{1,0:T(8,128)}) %all-reduce.4.cloned.1.call-update) | async-done | bytes 524304 | tf_op jit(solution)/shard_map/psum | solution.py:185
  (237 shorter events, 116.0 us)
Async XLA Ops:
  7.2 156.8 %copy-start = (bf16[1,768,2048]{2,1,0:T(8,128)(2,1)S(1)}, bf16[1,768,2048]{2,1,0:T(8,128)(2,1)}, u32[]{:S(2)}) copy-start(bf16[1,768,2048]{2,1,0:T(8,128)(2,1)} %param.39) | copy-start | bytes 9437188
  7.2 7.4 %copy-start.60 = (f32[128,8]{0,1:T(8,128)S(1)}, f32[128,8]{0,1:T(8,128)}, u32[]{:S(2)}) copy-start(f32[128,8]{0,1:T(8,128)} %param.36) | copy-start | bytes 12292
  36.2 113.6 %all-to-all-start = ((bf16[128,10,2048]{2,1,0:T(8,128)(2,1)}), bf16[128,10,2048]{2,1,0:T(8,128)(2,1)}, u32[]{:S(2)}, u32[]{:S(2)}) async-start(bf16[128,10,2048]{2,1,0:T(8,128)(2,1)} %reshape.411), calls=%async_computation | async-start | bytes 16777216 | tf_op jit(solution)/shard_map/all_to_all | solution.py:80
  54.9 104.8 %copy-start.53 = (bf16[1,64,2048]{2,1,0:T(8,128)(2,1)S(1)}, bf16[1,64,2048]{2,1,0:T(8,128)(2,1)}, u32[]{:S(2)}) copy-start(bf16[1,64,2048]{2,1,0:T(8,128)(2,1)} %param.41) | copy-start | bytes 786436
  164.0 8.1 %slice-start.4 = ((s8[6291456]{0:T(1024)(128)(4,1)}), s8[4194304]{0:T(1024)(128)(4,1)S(1)}, s32[]{:S(2)}) async-start(s8[6291456]{0:T(1024)(128)(4,1)} %bitcast.381), calls=%async_computation.12 | async-start | bytes 8388608
  191.9 116.3 %all-to-all-start.1 = ((bf16[128,10,2048]{2,1,0:T(8,128)(2,1)}), bf16[128,10,2048]{2,1,0:T(8,128)(2,1)}, u32[]{:S(2)}, u32[]{:S(2)}) async-start(bf16[128,10,2048]{2,1,0:T(8,128)(2,1)} %reshape.413), calls=%async_computation.1 | async-start | bytes 16777216 | tf_op jit(solution)/shard_map/all_to_all | solution.py:90
  206.9 187.7 %all-gather.2.cloned.1.call-start = ((), (), s32[]{:S(2)}) async-start(), calls=%async_computation.4 | async-start | bytes 8912896 | tf_op jit(solution)/shard_map/all_gather | solution.py:102
  335.1 11.0 %copy-start.38 = (bf16[2048,256]{1,0:T(8,128)(2,1)S(1)}, bf16[2048,256]{1,0:T(8,128)(2,1)}, u32[]{:S(2)}) copy-start(bf16[2048,256]{1,0:T(8,128)(2,1)} %param.42) | copy-start | bytes 3145732
  336.1 176.4 %reduce-scatter.3.cloned.1.call-start = ((), (), s32[]{:S(2)}) async-start(), calls=%async_computation.6 | async-start | bytes 2228224 | tf_op jit(solution)/shard_map/reduce_scatter | solution.py:190
  348.0 8.0 %copy-start.45 = (bf16[512,256]{0,1:T(8,128)(2,1)}, bf16[512,256]{0,1:T(8,128)(2,1)S(1)}, u32[]{:S(2)}) copy-start(bf16[512,256]{0,1:T(8,128)(2,1)S(1)} %copy.185) | copy-start | bytes 786436
  348.1 10.8 %copy-start.36 = (bf16[1024,128]{0,1:T(8,128)(2,1)}, bf16[1024,128]{0,1:T(8,128)(2,1)S(1)}, u32[]{:S(2)}) copy-start(bf16[1024,128]{0,1:T(8,128)(2,1)S(1)} %copy.189) | copy-start | bytes 786436
  348.3 15.8 %copy-start.32 = (bf16[512,256]{0,1:T(8,128)(2,1)}, bf16[512,256]{0,1:T(8,128)(2,1)S(1)}, u32[]{:S(2)}) copy-start(bf16[512,256]{0,1:T(8,128)(2,1)S(1)} %copy.186) | copy-start | bytes 786436
  348.5 25.5 %copy-start.30 = (bf16[1536,128]{0,1:T(8,128)(2,1)}, bf16[1536,128]{0,1:T(8,128)(2,1)S(1)}, u32[]{:S(2)}) copy-start(bf16[1536,128]{0,1:T(8,128)(2,1)S(1)} %copy.190) | copy-start | bytes 1179652
  349.5 10.8 %copy-start.39 = (bf16[512,256]{0,1:T(8,128)(2,1)}, bf16[512,256]{0,1:T(8,128)(2,1)S(1)}, u32[]{:S(2)}) copy-start(bf16[512,256]{0,1:T(8,128)(2,1)S(1)} %copy.184) | copy-start | bytes 786436
  358.9 11.3 %copy-start.10 = (bf16[2,512,1024]{1,2,0:T(8,128)(2,1)}, bf16[2,512,1024]{1,2,0:T(8,128)(2,1)S(1)}, u32[]{:S(2)}) copy-start(bf16[2,512,1024]{1,2,0:T(8,128)(2,1)S(1)} %fusion.67) | copy-start | bytes 6291460
  387.1 6.7 copy-start.16
  405.0 7.3 %copy-start.48 = (bf16[512,256]{0,1:T(8,128)(2,1)}, bf16[512,256]{0,1:T(8,128)(2,1)S(1)}, u32[]{:S(2)}) copy-start(bf16[512,256]{0,1:T(8,128)(2,1)S(1)} %get-tuple-element.154) | copy-start | bytes 786436
  410.5 9.6 %copy-start.6 = (bf16[2,512,2048]{1,2,0:T(8,128)(2,1)}, bf16[2,512,2048]{1,2,0:T(8,128)(2,1)S(1)}, u32[]{:S(2)}) copy-start(bf16[2,512,2048]{1,2,0:T(8,128)(2,1)S(1)} %fusion.5) | copy-start | bytes 12582916
  422.2 134.4 %reduce-scatter.5.cloned.1.call-start = ((), (), s32[]{:S(2)}) async-start(), calls=%async_computation.7 | async-start | bytes 2228224 | tf_op jit(solution)/shard_map/reduce_scatter | solution.py:193
  433.7 276.3 %all-reduce.4.cloned.1.call-start = ((), (), s32[]{:S(2)}) async-start(), calls=%async_computation.5 | async-start | bytes 1048576 | tf_op jit(solution)/shard_map/psum | solution.py:185
  436.7 50.8 %copy-start.19 = (bf16[2,512,512]{1,2,0:T(8,128)(2,1)S(1)}, bf16[2,512,512]{1,2,0:T(8,128)(2,1)}, u32[]{:S(2)}) copy-start(bf16[2,512,512]{1,2,0:T(8,128)(2,1)} %copy-done.18) | copy-start | bytes 3145732
  442.1 47.4 %copy-start.13 = (bf16[2,512,1024]{1,2,0:T(8,128)(2,1)S(1)}, bf16[2,512,1024]{1,2,0:T(8,128)(2,1)}, u32[]{:S(2)}) copy-start(bf16[2,512,1024]{1,2,0:T(8,128)(2,1)} %copy-done.12) | copy-start | bytes 6291460
  446.9 47.0 %copy-start.57 = (bf16[512,64]{0,1:T(8,128)(2,1)S(1)}, bf16[512,64]{0,1:T(8,128)(2,1)}, u32[]{:S(2)}) copy-start(bf16[512,64]{0,1:T(8,128)(2,1)} %fusion.83) | copy-start | bytes 196612
  506.4 205.6 %copy-start.1 = (bf16[1,768,2048]{2,1,0:T(8,128)(2,1)S(1)}, bf16[1,768,2048]{2,1,0:T(8,128)(2,1)}, u32[]{:S(2)}) copy-start(bf16[1,768,2048]{2,1,0:T(8,128)(2,1)} %param.39) | copy-start | bytes 9437188
  (49 other events, 160.9 us)
Sparse Core Ops, SparseCore 0:
  336.2 57.9 all-gather.1
  422.3 67.4 reduce-scatter.2
  492.3 64.2 reduce-scatter.4
  561.8 148.2 all-reduce.3
where the time goes:
time: 727 us; the launch traced here: 719 us
  waiting for transfers between devices  391 us (54%)
  matrix products  108 us (15%)
  local copies, waits for them, and re-layouts  84 us (12%)
  other arithmetic  45.6 us (6%)
  blocking collectives  38.8 us (5%)
  starting transfers between devices  36.4 us (5%)
  between operations  14.9 us (2%)
    psum x1, waiting for transfers between devices, on_device(): lax.psum(adapter_scale * column_contrib, ('grp', 'dev'))  152 us
    all_to_all x1, waiting for transfers between devices, on_device(): lax.all_to_all(grad_rows.reshape(experts, capacity, model_width), ('grp',...  101 us
    all_to_all x1, waiting for transfers between devices, on_device(): lax.all_to_all(outgoing, ('grp', 'dev'), split_axis=0, concat_axis=0, til...  94.9 us
    reduce_scatter x1, waiting for transfers between devices, on_device(): lax.psum_scatter(value_term.astype(jnp.bfloat16), 'dev', scatter_dimensio...  42.5 us
    dot_general x11, matrix products, contraction(): lax.dot_general(left, right, (((left_dim,), (right_dim,)), ((), ())), pre...  40.8 us
    psum x1, blocking collectives, on_device(): lax.psum((adapter_scale * row_contrib).astype(jnp.bfloat16), 'grp')  38.8 us
    unnamed x146, local copies, waits for them, and re-layouts  28.2 us
    sub x4, matrix products, on_device(): probs_full = jnp.exp(scores - jnp.max(scores, axis=2, keepdims=True))  22 us
  transfers between devices with their start and end apart: 6, of which 4 were waited for; matrix products, arithmetic and copies ran while one was open for 15% of the time, Pallas kernels for 0%

commit v1 on v0

--- a/solution.py
+++ b/solution.py
@@ -182,7 +182,9 @@
     output_first_gradient = lax.psum(
         (adapter_scale * row_contrib).astype(jnp.bfloat16), "grp"
     ).astype(jnp.float32)
-    output_second_gradient = lax.psum(adapter_scale * column_contrib, ("grp", "dev"))
+    output_second_gradient = jnp.sum(
+        lax.all_gather(adapter_scale * column_contrib, ("grp", "dev")), axis=0
+    )
     empty = jnp.zeros((piece_len, KVH * HEAD_SIZE), jnp.float32)
     key_term = lax.dynamic_update_slice(empty, grad_key_sum, (0, kv_index * HEAD_SIZE))
     value_term = lax.dynamic_update_slice(empty, grad_value_sum, (0, kv_index * HEAD_SIZE))

time: 727 us -> 960 us (1.32)
  waiting for transfers between devices: 391 us -> 616 us
  other arithmetic: 45.6 us -> 63.7 us
    all_gather x0 -> x1, waiting for transfers between devices: none -> 370 us  [on_device(): lax.all_gather(adapter_scale * column_contrib, ('grp', 'dev'))]
    psum x1 -> x0, waiting for transfers between devices: 152 us -> none  [on_device(): lax.psum(adapter_scale * column_contrib, ('grp', 'dev'))]
    reduce_scatter x1, waiting for transfers between devices: 42.5 us -> 0.01 us  [on_device(): lax.psum_scatter(value_term.astype(jnp.bfloat16), 'dev', scatter_dimensio...]
    reduce_scatter x1, waiting for transfers between devices: 0.01 us -> 42 us  [on_device(): lax.psum_scatter(key_term.astype(jnp.bfloat16), 'dev', scatter_dimension=...]
    reduce_sum x0 -> x1, other arithmetic: none -> 21.8 us  [on_device(): jnp.sum(lax.all_gather(adapter_scale * column_contrib, ('grp', 'dev')), a...]
    all_to_all x1, starting transfers between devices: 12.4 us -> 23.5 us  [on_device(): lax.all_to_all(outgoing, ('grp', 'dev'), split_axis=0, concat_axis=0, til...]
    unnamed x146 -> x135, local copies, waits for them, and re-layouts: 28.2 us -> 23.9 us
  transfers between devices with their start and end apart: 6 -> 6, of which waited for: 4 -> 5; matrix products, arithmetic and copies ran while one was open for 15% -> 11% of each run, Pallas kernels for 0% -> 0%
where the time goes in v1:
time: 960 us; the launch traced here: 952 us
  waiting for transfers between devices  616 us (64%)
  matrix products  102 us (11%)
  local copies, waits for them, and re-layouts  80.1 us (8%)
  other arithmetic  63.7 us (7%)
  starting transfers between devices  39.3 us (4%)
  blocking collectives  34.9 us (4%)
  between operations  15 us (2%)
    all_gather x1, waiting for transfers between devices, on_device(): lax.all_gather(adapter_scale * column_contrib, ('grp', 'dev'))  370 us
    all_to_all x1, waiting for transfers between devices, on_device(): lax.all_to_all(grad_rows.reshape(experts, capacity, model_width), ('grp',...  101 us
    all_to_all x1, waiting for transfers between devices, on_device(): lax.all_to_all(outgoing, ('grp', 'dev'), split_axis=0, concat_axis=0, til...  94.9 us
    reduce_scatter x1, waiting for transfers between devices, on_device(): lax.psum_scatter(key_term.astype(jnp.bfloat16), 'dev', scatter_dimension=...  42 us
    dot_general x11, matrix products, contraction(): lax.dot_general(left, right, (((left_dim,), (right_dim,)), ((), ())), pre...  36.5 us
    psum x1, blocking collectives, on_device(): lax.psum((adapter_scale * row_contrib).astype(jnp.bfloat16), 'grp')  34.9 us
    unnamed x135, local copies, waits for them, and re-layouts  23.9 us
    all_to_all x1, starting transfers between devices, on_device(): lax.all_to_all(outgoing, ('grp', 'dev'), split_axis=0, concat_axis=0, til...  23.5 us
  transfers between devices with their start and end apart: 6, of which 5 were waited for; matrix products, arithmetic and copies ran while one was open for 11% of the time, Pallas kernels for 0%

profile of v1, /device:TPU:1, one launch (start us, length us, event | category | flops | bytes accessed | tf_op | source)
XLA Modules:
  0.0 951.7 jit_solution(671298067243799853)
XLA Ops:
  16.1 10.5 %scatter_custom_fusion = bf16[1280,2048]{1,0:T(8,128)(2,1)} fusion(s32[1024]{0:T(1024)S(1)} %bitcast.380, f32[128,2048]{1,0:T(8,128)} %convert_element_type.174, f32[1024]{0:T(1024)S(1)} %mul.209, bf16[]{:T(256)} %constant.250.clone.1), kind=kCustom, calls=%fused_computation.28 | custom fusion | flops 4194304 | bytes 6295554 | tf_op jit(solution)/shard_map/scatter | solution.py:78
  26.5 9.5 %reshape.411 = bf16[128,10,2048]{2,1,0:T(8,128)(2,1)} reshape(bf16[1280,2048]{1,0:T(8,128)(2,1)} %scatter_custom_fusion) | data formatting | bytes 10485760 | tf_op jit(solution)/shard_map/reshape | solution.py:79
  36.1 23.5 %all-to-all-start = ((bf16[128,10,2048]{2,1,0:T(8,128)(2,1)}), bf16[128,10,2048]{2,1,0:T(8,128)(2,1)}, u32[]{:S(2)}, u32[]{:S(2)}) async-start(bf16[128,10,2048]{2,1,0:T(8,128)(2,1)} %reshape.411), calls=%async_computation | async-start | bytes 16777216 | tf_op jit(solution)/shard_map/all_to_all | solution.py:80
  59.6 6.3 copy.100
  65.9 94.9 %all-to-all-done = bf16[128,10,2048]{2,1,0:T(8,128)(2,1)} async-done(((bf16[128,10,2048]{2,1,0:T(8,128)(2,1)}), bf16[128,10,2048]{2,1,0:T(8,128)(2,1)}, u32[]{:S(2)}, u32[]{:S(2)}) %all-to-all-start) | async-done | bytes 5242912 | tf_op jit(solution)/shard_map/all_to_all | solution.py:80
  160.8 9.8 %reshape.412 = bf16[1280,2048]{1,0:T(8,128)(2,1)} reshape(bf16[128,10,2048]{2,1,0:T(8,128)(2,1)} %all-to-all-done) | data formatting | bytes 10485760 | tf_op jit(solution)/shard_map/reshape | solution.py:81
  183.2 10.2 %convolution_convert_fusion = bf16[1280,2048]{1,0:T(8,128)(2,1)} fusion(bf16[1,2048,1536]{2,1,0:T(8,128)(2,1)S(1)} %bitcast.383, bf16[1280,768]{0,1:T(8,128)(2,1)S(1)} %get-tuple-element.149, bf16[1280,768]{0,1:T(8,128)(2,1)S(1)} %get-tuple-element.148), kind=kOutput, calls=%fused_computation.14 | convolution fusion | flops 8063549440 | bytes 15466496 | tf_op jit(solution)/shard_map/dot_general | solution.py:14
  193.4 9.5 %reshape.413 = bf16[128,10,2048]{2,1,0:T(8,128)(2,1)} reshape(bf16[1280,2048]{1,0:T(8,128)(2,1)} %convolution_convert_fusion) | data formatting | bytes 10485760 | tf_op jit(solution)/shard_map/reshape | solution.py:91
  202.9 15.0 %all-to-all-start.1 = ((bf16[128,10,2048]{2,1,0:T(8,128)(2,1)}), bf16[128,10,2048]{2,1,0:T(8,128)(2,1)}, u32[]{:S(2)}, u32[]{:S(2)}) async-start(bf16[128,10,2048]{2,1,0:T(8,128)(2,1)} %reshape.413), calls=%async_computation.1 | async-start | bytes 16777216 | tf_op jit(solution)/shard_map/all_to_all | solution.py:90
  218.0 101.3 %all-to-all-done.1 = bf16[128,10,2048]{2,1,0:T(8,128)(2,1)} async-done(((bf16[128,10,2048]{2,1,0:T(8,128)(2,1)}), bf16[128,10,2048]{2,1,0:T(8,128)(2,1)}, u32[]{:S(2)}, u32[]{:S(2)}) %all-to-all-start.1) | async-done | bytes 5242912 | tf_op jit(solution)/shard_map/all_to_all | solution.py:90
  319.3 9.8 %reshape.414 = bf16[1280,2048]{1,0:T(8,128)(2,1)} reshape(bf16[128,10,2048]{2,1,0:T(8,128)(2,1)} %all-to-all-done.1) | data formatting | bytes 10485760 | tf_op jit(solution)/shard_map/reshape | solution.py:97
  329.1 12.0 %gather_fusion = bf16[1024,2048]{1,0:T(8,128)(2,1)} fusion(bf16[1280,2048]{1,0:T(8,128)(2,1)} %reshape.414, s32[1024]{0:T(1024)S(1)} %broadcast_clamp_fusion), kind=kCustom, calls=%fused_computation | custom fusion | bytes 8392704 | tf_op jit(solution)/shard_map/gather | solution.py:97
  341.1 5.1 convert_reduce_fusion
  356.7 4.7 fusion.177
  366.5 6.1 fusion.178
  381.4 8.2 fusion.179
  389.6 4.7 fusion.33
  397.1 8.1 all-gather.4.cloned.1.call-done
  405.3 6.2 convolution_convert_fusion.2
  456.7 5.3 fusion.54
  472.3 34.9 %psum.7 = bf16[64,256]{1,0:T(8,128)(2,1)S(1)} all-reduce(bf16[64,256]{1,0:T(8,128)(2,1)S(1)} %fusion.88), channel_id=1, replica_groups=mesh['grp'=8,'dev'=16] {'grp'}, use_global_device_ids=true, to_apply=%region_13.14 | all-reduce | flops 16384 | bytes 65536 | tf_op jit(solution)/shard_map/psum | solution.py:182
  509.5 42.0 %reduce-scatter.3.cloned.1.call-done = bf16[128,512]{1,0:T(8,128)(2,1)} async-done(((bf16[2048,512]{1,0:T(8,128)(2,1)}), bf16[128,512]{1,0:T(8,128)(2,1)}) %reduce-scatter.3.cloned.1.call-update) | async-done | bytes 131088 | tf_op jit(solution)/shard_map/reduce_scatter | solution.py:192
  553.1 370.1 %all-gather.6.cloned.1.call-done = f32[8192,2048]{1,0:T(8,128)} async-done(((f32[64,2048]{1,0:T(8,128)}), f32[8192,2048]{1,0:T(8,128)}) %all-gather.6.cloned.1.call-update) | async-done | bytes 67108880 | tf_op jit(solution)/shard_map/all_gather | solution.py:186
  923.2 21.8 %reduce_sum.148 = f32[64,2048]{1,0:T(8,128)} reduce(f32[128,64,2048]{2,1,0:T(8,128)} %bitcast.38, f32[]{:T(128)} %constant.256.clone.1), dimensions={0}, to_apply=%region_18.19 | reduce | flops 16646144 | bytes 67633152 | tf_op jit(solution)/shard_map/reduce_sum | solution.py:185
  (227 shorter events, 107.2 us)
Async XLA Ops:
  7.2 167.8 %copy-start = (bf16[1,768,2048]{2,1,0:T(8,128)(2,1)S(1)}, bf16[1,768,2048]{2,1,0:T(8,128)(2,1)}, u32[]{:S(2)}) copy-start(bf16[1,768,2048]{2,1,0:T(8,128)(2,1)} %param.39) | copy-start | bytes 9437188
  7.2 7.3 copy-start.54
  36.1 124.7 %all-to-all-start = ((bf16[128,10,2048]{2,1,0:T(8,128)(2,1)}), bf16[128,10,2048]{2,1,0:T(8,128)(2,1)}, u32[]{:S(2)}, u32[]{:S(2)}) async-start(bf16[128,10,2048]{2,1,0:T(8,128)(2,1)} %reshape.411), calls=%async_computation | async-start | bytes 16777216 | tf_op jit(solution)/shard_map/all_to_all | solution.py:80
  65.9 104.7 %copy-start.51 = (bf16[1,64,2048]{2,1,0:T(8,128)(2,1)S(1)}, bf16[1,64,2048]{2,1,0:T(8,128)(2,1)}, u32[]{:S(2)}) copy-start(bf16[1,64,2048]{2,1,0:T(8,128)(2,1)} %param.41) | copy-start | bytes 786436
  170.6 4.4 copy-start.4
  175.0 8.1 slice-start.4
  202.9 116.3 %all-to-all-start.1 = ((bf16[128,10,2048]{2,1,0:T(8,128)(2,1)}), bf16[128,10,2048]{2,1,0:T(8,128)(2,1)}, u32[]{:S(2)}, u32[]{:S(2)}) async-start(bf16[128,10,2048]{2,1,0:T(8,128)(2,1)} %reshape.413), calls=%async_computation.1 | async-start | bytes 16777216 | tf_op jit(solution)/shard_map/all_to_all | solution.py:90
  217.9 187.3 %all-gather.4.cloned.1.call-start = ((), (), s32[]{:S(2)}) async-start(), calls=%async_computation.4 | async-start | bytes 8912896 | tf_op jit(solution)/shard_map/all_gather | solution.py:102
  341.1 5.1 copy-start.27
  347.1 160.7 %reduce-scatter.5.cloned.1.call-start = ((), (), s32[]{:S(2)}) async-start(), calls=%async_computation.6 | async-start | bytes 2228224 | tf_op jit(solution)/shard_map/reduce_scatter | solution.py:195
  348.7 4.8 copy-start.12
  349.7 7.0 copy-start.38
  350.9 10.5 %copy-start.44 = (bf16[512,256]{0,1:T(8,128)(2,1)}, bf16[512,256]{0,1:T(8,128)(2,1)S(1)}, u32[]{:S(2)}) copy-start(bf16[512,256]{0,1:T(8,128)(2,1)S(1)} %copy.185) | copy-start | bytes 786436
  351.1 15.4 %copy-start.32 = (bf16[512,256]{0,1:T(8,128)(2,1)}, bf16[512,256]{0,1:T(8,128)(2,1)S(1)}, u32[]{:S(2)}) copy-start(bf16[512,256]{0,1:T(8,128)(2,1)S(1)} %copy.186) | copy-start | bytes 786436
  352.1 24.3 %copy-start.28 = (bf16[1536,128]{0,1:T(8,128)(2,1)}, bf16[1536,128]{0,1:T(8,128)(2,1)S(1)}, u32[]{:S(2)}) copy-start(bf16[1536,128]{0,1:T(8,128)(2,1)S(1)} %copy.190) | copy-start | bytes 1179652
  352.3 12.2 %copy-start.34 = (bf16[1024,128]{0,1:T(8,128)(2,1)}, bf16[1024,128]{0,1:T(8,128)(2,1)S(1)}, u32[]{:S(2)}) copy-start(bf16[1024,128]{0,1:T(8,128)(2,1)S(1)} %copy.189) | copy-start | bytes 786436
  364.5 8.1 copy-start.8
  389.6 6.8 copy-start.13
  405.3 6.2 copy-start.5
  405.3 6.2 copy-start.55
  422.3 129.1 %reduce-scatter.3.cloned.1.call-start = ((), (), s32[]{:S(2)}) async-start(), calls=%async_computation.5 | async-start | bytes 2228224 | tf_op jit(solution)/shard_map/reduce_scatter | solution.py:192
  440.8 482.4 %all-gather.6.cloned.1.call-start = ((), (), s32[]{:S(2)}) async-start(), calls=%async_computation.7 | async-start | bytes 67633152 | tf_op jit(solution)/shard_map/all_gather | solution.py:186
  448.6 8.1 copy-start.53
  923.2 21.8 %copy-start.1 = (bf16[1,768,2048]{2,1,0:T(8,128)(2,1)S(1)}, bf16[1,768,2048]{2,1,0:T(8,128)(2,1)}, u32[]{:S(2)}) copy-start(bf16[1,768,2048]{2,1,0:T(8,128)(2,1)} %param.39) | copy-start | bytes 9437188
  (44 other events, 118.9 us)
Sparse Core Ops, SparseCore 0:
  347.2 57.9 all-gather.3
  422.5 62.3 reduce-scatter.4
  487.3 64.1 reduce-scatter.2
  553.6 369.5 all-gather.5
